TPU v7x, 32 devices: a whole 2x2x4 slice. The times are simulated.
32 devices in a mesh: dp: 4 (over z), seqhi: 2 (over x), seqlo: 4 (over y, core).
Axes of the slice: x: 2, y: 2, z: 4, core: 2. Of those that a mesh axis runs over, the one named last changes fastest.
Arguments:
- queries: bfloat16 [4, 2048, 384], P('dp', ('seqhi', 'seqlo')), may hold values from -2 to 2
- key_rows: bfloat16 [4, 2048, 384], P('dp', ('seqhi', 'seqlo')), may hold values from -2 to 2
- value_rows: bfloat16 [4, 2048, 384], P('dp', ('seqhi', 'seqlo')), may hold values from -3 to 3
- head_scale: float32 [6], replicated, may hold values from 0.15 to 1
- out_weight: bfloat16 [384, 384], replicated, may hold values from -0.3125 to 0.3125
- cotangent: bfloat16 [4, 2048, 384], P('dp', ('seqhi', 'seqlo')), may hold values from -6 to 6
Outputs:
- queries_gradient: bfloat16 [4, 2048, 384], P('dp', ('seqhi', 'seqlo'))
- keys_gradient: bfloat16 [4, 2048, 384], P('dp', ('seqhi', 'seqlo'))
- values_gradient: bfloat16 [4, 2048, 384], P('dp', ('seqhi', 'seqlo'))
- weight_gradient: float32 [384, 384], P('dp')
All inputs are finite; a program needn't handle non-finite values.
Results may differ from a plain program's by a relative error of at most 0.025.
Values may be sent and summed in bfloat16 or wider, within the bound.
No kernel may reach another device: no remote copies, remote signals or barrier semaphores. Data moves between devices by JAX's collectives and lax.ppermute only.
A program may use at most 64 MiB of HBM per device.

v0:
```python
import jax
import jax.numpy as jnp
from jax import lax
from jax.sharding import PartitionSpec as P


def swapped(value, axis, stride):
    mask = 2**stride
    pairs = [(source, source ^ mask) for source in range(lax.axis_size(axis))]
    return lax.ppermute(value, axis, pairs)


def split_heads(matrix, head_count):
    return matrix.reshape(matrix.shape[0], head_count, matrix.shape[1] // head_count)


def pair_mean(matrix):
    paired = matrix.astype(jnp.float32).reshape(matrix.shape[0] // 2, 2, matrix.shape[1])
    return (0.5 * (paired[:, 0] + paired[:, 1])).astype(jnp.bfloat16)


def pair_total(matrix):
    paired = matrix.astype(jnp.float32).reshape(matrix.shape[0] // 2, 2, matrix.shape[1])
    return (paired[:, 0] + paired[:, 1]).astype(jnp.bfloat16)


def spread_rows(matrix, factor):
    widened = jnp.broadcast_to(matrix[:, None], (matrix.shape[0], factor) + matrix.shape[1:])
    return widened.reshape((matrix.shape[0] * factor,) + matrix.shape[1:])


def group_sum(matrix, factor):
    return jnp.sum(matrix.reshape((matrix.shape[0] // factor, factor) + matrix.shape[1:]), axis=1)


def score_terms(queries, key_block, scales):
    head_count = scales.shape[0]
    factor = scales / jnp.sqrt(jnp.float32(queries.shape[1] // head_count))
    logits = jnp.einsum(
        "rhe,che->hrc",
        split_heads(queries, head_count),
        split_heads(key_block, head_count),
        preferred_element_type=jnp.float32,
    )
    return (jnp.exp(logits * factor[:, None, None]), factor)


def attend(queries, key_block, value_block, scales, multiplicity):
    head_count = scales.shape[0]
    weights, factor = score_terms(queries, key_block, scales)
    probabilities = weights.astype(jnp.bfloat16)
    numerator = jnp.einsum(
        "hrc,che->rhe",
        probabilities,
        split_heads(value_block, head_count),
        preferred_element_type=jnp.float32,
    )
    numerator = numerator.reshape(queries.shape[0], queries.shape[1])
    denominator = multiplicity * jnp.sum(weights, axis=2).T
    return (numerator, denominator)


def attend_back(queries, key_block, value_block, scales, multiplicity, numer_grad, denom_grad):
    head_count = scales.shape[0]
    weights, factor = score_terms(queries, key_block, scales)
    probabilities = weights.astype(jnp.bfloat16)
    grad_heads = split_heads(numer_grad, head_count)
    prob_grad = jnp.einsum(
        "rhe,che->hrc",
        grad_heads,
        split_heads(value_block, head_count),
        preferred_element_type=jnp.float32,
    )
    logit_grad = (
        weights * (prob_grad + multiplicity * denom_grad.T[:, :, None]) * factor[:, None, None]
    ).astype(jnp.bfloat16)
    query_piece = jnp.einsum(
        "hrc,che->rhe",
        logit_grad,
        split_heads(key_block, head_count),
        preferred_element_type=jnp.float32,
    ).reshape(queries.shape)
    key_piece = jnp.einsum(
        "hrc,rhe->che",
        logit_grad,
        split_heads(queries, head_count),
        preferred_element_type=jnp.float32,
    ).reshape(key_block.shape)
    value_piece = jnp.einsum(
        "hrc,rhe->che", probabilities, grad_heads, preferred_element_type=jnp.float32
    ).reshape(value_block.shape)
    return (query_piece, key_piece, value_piece)


def shards(queries, key_rows, value_rows, head_scale, out_weight, cotangent):
    query_local = queries[0]
    key_local = key_rows[0]
    value_local = value_rows[0]
    cotan_local = cotangent[0]
    head_count = head_scale.shape[0]
    feature_width = query_local.shape[1]
    block_rows = key_local.shape[0] // 2
    top_level = lax.axis_size(("seqhi", "seqlo")).bit_length() - 1
    position = lax.axis_index(("seqhi", "seqlo"))
    numerator, denominator = attend(query_local, key_local, value_local, head_scale, 1.0)
    coarse_queries = [query_local]
    sibling_pairs = [None]
    level_numers = [None]
    level_denoms = [None]
    own_keys = pair_mean(key_local)
    own_values = pair_total(value_local)
    for height in range(1, top_level + 1):
        coarse_queries.append(pair_mean(coarse_queries[-1]))
        if height > 1:
            lower_first = position // 2 ** (height - 2) % 2 == 0
            sib_keys, sib_values = sibling_pairs[-1]
            own_keys = pair_mean(
                jnp.concatenate(
                    [
                        jnp.where(lower_first, own_keys, sib_keys),
                        jnp.where(lower_first, sib_keys, own_keys),
                    ],
                    axis=0,
                )
            )
            own_values = pair_total(
                jnp.concatenate(
                    [
                        jnp.where(lower_first, own_values, sib_values),
                        jnp.where(lower_first, sib_values, own_values),
                    ],
                    axis=0,
                )
            )
        arrived = swapped((own_keys, own_values), ("seqhi", "seqlo"), height - 1)
        sibling_pairs.append(arrived)
        level_numer, level_denom = attend(
            coarse_queries[height], arrived[0], arrived[1], head_scale, float(2**height)
        )
        level_numers.append(level_numer)
        level_denoms.append(level_denom)
    numer_acc = level_numers[top_level]
    denom_acc = level_denoms[top_level]
    for height in range(top_level - 1, 0, -1):
        numer_acc = level_numers[height] + spread_rows(numer_acc, 2)
        denom_acc = level_denoms[height] + spread_rows(denom_acc, 2)
    numerator = numerator + spread_rows(numer_acc, 2)
    denominator = denominator + spread_rows(denom_acc, 2)
    attended_heads = split_heads(numerator, head_count) / denominator[:, :, None]
    attended = attended_heads.reshape(numerator.shape).astype(jnp.bfloat16)
    own_rows = feature_width // lax.axis_size("dp")
    weight_term = lax.dot_general(
        attended, cotan_local, (((0,), (0,)), ((), ())), preferred_element_type=jnp.float32
    )
    summed = lax.psum(weight_term, ("dp", "seqhi", "seqlo"))
    weight_gradient = lax.dynamic_slice_in_dim(summed, lax.axis_index("dp") * own_rows, own_rows, 0)
    backward = lax.dot_general(
        cotan_local, out_weight, (((1,), (1,)), ((), ())), preferred_element_type=jnp.float32
    ).astype(jnp.bfloat16)
    back_heads = split_heads(backward, head_count).astype(jnp.float32)
    numer_grad = (back_heads / denominator[:, :, None]).reshape(numerator.shape)
    denom_grad = -jnp.sum(back_heads * attended_heads, axis=2) / denominator
    query_grad, key_grad, value_grad = attend_back(
        query_local,
        key_local,
        value_local,
        head_scale,
        1.0,
        numer_grad.astype(jnp.bfloat16),
        denom_grad,
    )
    level_query_grads = [None]
    level_key_sends = [None]
    numer_group = numer_grad
    denom_group = denom_grad
    for height in range(1, top_level + 1):
        numer_group = group_sum(numer_group, 2)
        denom_group = group_sum(denom_group, 2)
        query_piece, key_piece, value_piece = attend_back(
            coarse_queries[height],
            sibling_pairs[height][0],
            sibling_pairs[height][1],
            head_scale,
            float(2**height),
            numer_group.astype(jnp.bfloat16),
            denom_group,
        )
        level_query_grads.append(query_piece)
        level_key_sends.append((key_piece, value_piece))
    chain_query = level_query_grads[top_level]
    for height in range(top_level - 1, 0, -1):
        chain_query = level_query_grads[height] + spread_rows(0.5 * chain_query, 2)
    query_total = query_grad + spread_rows(0.5 * chain_query, 2)
    returned = [None]
    for height in range(1, top_level + 1):
        returned.append(swapped(level_key_sends[height], ("seqhi", "seqlo"), height - 1))
    carry_pair = returned[top_level]
    for height in range(top_level - 1, 0, -1):
        up_keys = spread_rows(0.5 * carry_pair[0], 2)
        up_values = spread_rows(carry_pair[1], 2)
        split_lower_first = position // 2 ** (height - 1) % 2 == 0
        own_pair = (
            jnp.where(split_lower_first, up_keys[:block_rows], up_keys[block_rows:]),
            jnp.where(split_lower_first, up_values[:block_rows], up_values[block_rows:]),
        )
        other_pair = (
            jnp.where(split_lower_first, up_keys[block_rows:], up_keys[:block_rows]),
            jnp.where(split_lower_first, up_values[block_rows:], up_values[:block_rows]),
        )
        own_pair, other_pair = (own_pair, other_pair)
        parent = swapped((other_pair[0], other_pair[1]), ("seqhi", "seqlo"), height - 1)
        carry_pair = (
            own_pair[0] + parent[0] + returned[height][0],
            own_pair[1] + parent[1] + returned[height][1],
        )
    key_total = key_grad + spread_rows(0.5 * carry_pair[0], 2)
    value_total = value_grad + spread_rows(carry_pair[1], 2)
    return (
        query_total.astype(jnp.bfloat16)[None],
        key_total.astype(jnp.bfloat16)[None],
        value_total.astype(jnp.bfloat16)[None],
        weight_gradient,
    )


def solution(mesh):
    in_specs = (
        P("dp", ("seqhi", "seqlo"), None),
        P("dp", ("seqhi", "seqlo"), None),
        P("dp", ("seqhi", "seqlo"), None),
        P(),
        P(),
        P("dp", ("seqhi", "seqlo"), None),
    )
    out_specs = (
        P("dp", ("seqhi", "seqlo"), None),
        P("dp", ("seqhi", "seqlo"), None),
        P("dp", ("seqhi", "seqlo"), None),
        P("dp", None),
    )
    return jax.shard_map(shards, mesh=mesh, in_specs=in_specs, out_specs=out_specs, check_vma=False)
```

profile of v0, /device:TPU:1, one launch (start us, length us, event | category | flops | bytes accessed | tf_op | source)
XLA Modules:
  0.0 210.4 jit_solution(2963989376022502578)
XLA Ops:
  7.2 1.2 reshape.433
  15.5 2.3 %collective-permute-start.4 = (bf16[128,384]{1,0:T(8,128)(2,1)}, bf16[128,384]{1,0:T(8,128)(2,1)S(1)}, u32[]{:S(2)}, u32[]{:S(2)}) collective-permute-start(bf16[128,384]{1,0:T(8,128)(2,1)} %fusion.37), channel_id=1, source_target_pairs={{0,2},{1,3},{2,0},{3,1},{4,6},{5,7},{6,4},{7,5},{8,10},{9,11},{10,... | collective-permute-start | bytes 294920 | tf_op jit(solution)/shard_map/ppermute | solution.py:10
  22.9 1.1 collective-permute-start.5
  26.1 1.0 copy.302
  27.4 1.0 copy.325
  30.7 1.9 divide_convert_fusion
  35.3 1.0 copy.326
  38.0 1.5 reshape.410
  39.5 1.0 copy.330
  40.5 1.1 copy.315
  41.7 1.1 fusion.16
  46.2 1.4 div.55
  47.6 1.6 divide_reduce_fusion
  56.7 2.1 %fusion.30 = f32[384,384]{1,0:T(8,128)} fusion(bf16[256,384]{0,1:T(8,128)(2,1)} %bitcast.190, bf16[1,256,384]{2,1,0:T(8,128)(2,1)} %param.11), kind=kOutput, calls=%fused_computation.59 | convolution fusion | flops 75497472 | bytes 983040 | tf_op jit(solution)/shard_map/dot_general | solution.py:152
  62.3 2.4 %collective-permute-start.8 = (f32[128,384]{1,0:T(8,128)S(1)}, f32[128,384]{1,0:T(8,128)}, u32[]{:S(2)}, u32[]{:S(2)}) collective-permute-start(f32[128,384]{1,0:T(8,128)S(1)} %copy.351), channel_id=1, source_target_pairs={{0,2},{1,3},{2,0},{3,1},{4,6},{5,7},{6,4},{7,5},{8,10},{9,11},{10,... | collective-permute-start | bytes 589832 | tf_op jit(solution)/shard_map/ppermute | solution.py:10
  64.7 2.4 %collective-permute-start.10 = (f32[128,384]{1,0:T(8,128)S(1)}, f32[128,384]{1,0:T(8,128)}, u32[]{:S(2)}, u32[]{:S(2)}) collective-permute-start(f32[128,384]{1,0:T(8,128)S(1)} %copy.353), channel_id=1, source_target_pairs={{0,1},{1,0},{2,3},{3,2},{4,5},{5,4},{6,7},{7,6},{8,9},{9,8},{10,11... | collective-permute-start | bytes 589832 | tf_op jit(solution)/shard_map/ppermute | solution.py:10
  68.2 5.9 %collective-permute-done.6 = f32[128,384]{1,0:T(8,128)S(1)} collective-permute-done((f32[128,384]{1,0:T(8,128)}, f32[128,384]{1,0:T(8,128)S(1)}, u32[]{:S(2)}, u32[]{:S(2)}) %collective-permute-start.6) | collective-permute-done | bytes 196640 | tf_op jit(solution)/shard_map/ppermute | solution.py:10
  74.4 5.4 %collective-permute-done.11 = f32[128,384]{1,0:T(8,128)S(1)} collective-permute-done((f32[128,384]{1,0:T(8,128)S(1)}, f32[128,384]{1,0:T(8,128)S(1)}, u32[]{:S(2)}, u32[]{:S(2)}) %collective-permute-start.11) | collective-permute-done | bytes 196640 | tf_op jit(solution)/shard_map/ppermute | solution.py:10
  80.5 109.2 %all-reduce.2.cloned.1.call-done = f32[384,384]{1,0:T(8,128)} async-done(((f32[384,384]{1,0:T(8,128)}), f32[384,384]{1,0:T(8,128)}) %all-reduce.2.cloned.1.call-update) | async-done | bytes 589840 | tf_op jit(solution)/shard_map/psum | solution.py:155
  189.7 1.6 constant_dynamic-slice_fusion
  191.3 1.1 collective-permute-start.12
  194.4 3.2 %collective-permute-done.12 = f32[128,384]{1,0:T(8,128)} collective-permute-done((f32[128,384]{1,0:T(8,128)S(1)}, f32[128,384]{1,0:T(8,128)}, u32[]{:S(2)}, u32[]{:S(2)}) %collective-permute-start.12) | collective-permute-done | bytes 196640 | tf_op jit(solution)/shard_map/ppermute | solution.py:10
  197.6 1.1 add_add_fusion.1
  199.2 1.1 collective-permute-start.14
  (278 shorter events, 42.2 us)
Async XLA Ops:
  7.2 23.5 %copy-start = (bf16[384,384]{1,0:T(8,128)(2,1)S(1)}, bf16[384,384]{1,0:T(8,128)(2,1)}, u32[]{:S(2)}) copy-start(bf16[384,384]{1,0:T(8,128)(2,1)} %param.10) | copy-start | bytes 884740
  7.2 182.5 %all-reduce.2.cloned.1.call-start = ((), (), s32[]{:S(2)}) async-start(), calls=%async_computation | async-start | bytes 1179648 | tf_op jit(solution)/shard_map/psum | solution.py:155
  8.8 5.4 %collective-permute-start = (bf16[128,384]{1,0:T(8,128)(2,1)S(1)}, bf16[128,384]{1,0:T(8,128)(2,1)S(1)}, u32[]{:S(2)}, u32[]{:S(2)}) collective-permute-start(bf16[128,384]{1,0:T(8,128)(2,1)S(1)} %fusion.33), channel_id=1, source_target_pairs={{0,1},{1,0},{2,3},{3,2},{4,5},{5,4},{6,7},{7,6},{8,9},{9,8},{10,11... | collective-permute-start | bytes 294920 | tf_op jit(solution)/shard_map/ppermute | solution.py:10
  9.5 4.7 %collective-permute-start.3 = (bf16[128,384]{1,0:T(8,128)(2,1)S(1)}, bf16[128,384]{1,0:T(8,128)(2,1)S(1)}, u32[]{:S(2)}, u32[]{:S(2)}) collective-permute-start(bf16[128,384]{1,0:T(8,128)(2,1)S(1)} %fusion.36), channel_id=1, source_target_pairs={{0,1},{1,0},{2,3},{3,2},{4,5},{5,4},{6,7},{7,6},{8,9},{9,8},{10,11... | collective-permute-start | bytes 294920 | tf_op jit(solution)/shard_map/ppermute | solution.py:10
  11.8 7.4 %copy-start.22 = (bf16[128,1,384]{0,2,1:T(8,128)(2,1)}, bf16[128,1,384]{0,2,1:T(8,128)(2,1)S(1)}, u32[]{:S(2)}) copy-start(bf16[128,1,384]{0,2,1:T(8,128)(2,1)S(1)} %copy.296) | copy-start | bytes 294916
  12.0 17.5 %copy-start.40 = (f32[6]{0:T(128)}, f32[6]{0:T(128)S(1)}, u32[]{:S(2)}) copy-start(f32[6]{0:T(128)S(1)} %broadcast_multiply_fusion.1) | copy-start | bytes 76
  12.5 14.6 %copy-start.12 = (bf16[64,384]{0,1:T(8,128)(2,1)}, bf16[64,384]{0,1:T(8,128)(2,1)S(1)}, u32[]{:S(2)}) copy-start(bf16[64,384]{0,1:T(8,128)(2,1)S(1)} %copy.389) | copy-start | bytes 147460
  15.5 5.3 %collective-permute-start.4 = (bf16[128,384]{1,0:T(8,128)(2,1)}, bf16[128,384]{1,0:T(8,128)(2,1)S(1)}, u32[]{:S(2)}, u32[]{:S(2)}) collective-permute-start(bf16[128,384]{1,0:T(8,128)(2,1)} %fusion.37), channel_id=1, source_target_pairs={{0,2},{1,3},{2,0},{3,1},{4,6},{5,7},{6,4},{7,5},{8,10},{9,11},{10,... | collective-permute-start | bytes 294920 | tf_op jit(solution)/shard_map/ppermute | solution.py:10
  19.1 5.0 %collective-permute-start.1 = (bf16[128,384]{1,0:T(8,128)(2,1)}, bf16[128,384]{1,0:T(8,128)(2,1)}, u32[]{:S(2)}, u32[]{:S(2)}) collective-permute-start(bf16[128,384]{1,0:T(8,128)(2,1)} %fusion.34), channel_id=1, source_target_pairs={{0,2},{1,3},{2,0},{3,1},{4,6},{5,7},{6,4},{7,5},{8,10},{9,11},{10,... | collective-permute-start | bytes 294920 | tf_op jit(solution)/shard_map/ppermute | solution.py:10
  22.9 12.4 %collective-permute-start.5 = (bf16[128,384]{1,0:T(8,128)(2,1)}, bf16[128,384]{1,0:T(8,128)(2,1)}, u32[]{:S(2)}, u32[]{:S(2)}) collective-permute-start(bf16[128,384]{1,0:T(8,128)(2,1)} %bitcast.146), channel_id=1, source_target_pairs={{0,4},{1,5},{2,6},{3,7},{4,0},{5,1},{6,2},{7,3},{8,12},{9,13},{10,... | collective-permute-start | bytes 294920 | tf_op jit(solution)/shard_map/ppermute | solution.py:10
  25.3 4.3 %copy-start.35 = (bf16[32,6,64]{2,1,0:T(8,128)(2,1)S(1)}, bf16[32,6,64]{2,1,0:T(8,128)(2,1)}, u32[]{:S(2)}) copy-start(bf16[32,6,64]{2,1,0:T(8,128)(2,1)} %convert_element_type.251) | copy-start | bytes 73732
  25.6 3.8 %collective-permute-start.2 = (bf16[128,384]{1,0:T(8,128)(2,1)S(1)}, bf16[128,384]{1,0:T(8,128)(2,1)S(1)}, u32[]{:S(2)}, u32[]{:S(2)}) collective-permute-start(bf16[128,384]{1,0:T(8,128)(2,1)S(1)} %fusion.35), channel_id=1, source_target_pairs={{0,4},{1,5},{2,6},{3,7},{4,0},{5,1},{6,2},{7,3},{8,12},{9,13},{10,... | collective-permute-start | bytes 294920 | tf_op jit(solution)/shard_map/ppermute | solution.py:10
  29.8 6.5 %copy-start.7 = (f32[6,32,128]{2,1,0:T(8,128)}, f32[6,32,128]{2,1,0:T(8,128)S(1)}, u32[]{:S(2)}) copy-start(f32[6,32,128]{2,1,0:T(8,128)S(1)} %get-tuple-element.37) | copy-start | bytes 294916
  61.6 12.5 %copy-start.39 = (f32[128,384]{1,0:T(8,128)S(1)}, f32[128,384]{1,0:T(8,128)}, u32[]{:S(2)}) copy-start(f32[128,384]{1,0:T(8,128)} %copy.357) | copy-start | bytes 589828
  62.3 129.0 %collective-permute-start.8 = (f32[128,384]{1,0:T(8,128)S(1)}, f32[128,384]{1,0:T(8,128)}, u32[]{:S(2)}, u32[]{:S(2)}) collective-permute-start(f32[128,384]{1,0:T(8,128)S(1)} %copy.351), channel_id=1, source_target_pairs={{0,2},{1,3},{2,0},{3,1},{4,6},{5,7},{6,4},{7,5},{8,10},{9,11},{10,... | collective-permute-start | bytes 589832 | tf_op jit(solution)/shard_map/ppermute | solution.py:10
  64.7 135.6 %collective-permute-start.10 = (f32[128,384]{1,0:T(8,128)S(1)}, f32[128,384]{1,0:T(8,128)}, u32[]{:S(2)}, u32[]{:S(2)}) collective-permute-start(f32[128,384]{1,0:T(8,128)S(1)} %copy.353), channel_id=1, source_target_pairs={{0,1},{1,0},{2,3},{3,2},{4,5},{5,4},{6,7},{7,6},{8,9},{9,8},{10,11... | collective-permute-start | bytes 589832 | tf_op jit(solution)/shard_map/ppermute | solution.py:10
  67.0 134.6 %collective-permute-start.15 = (f32[128,384]{1,0:T(8,128)S(1)}, f32[128,384]{1,0:T(8,128)S(1)}, u32[]{:S(2)}, u32[]{:S(2)}) collective-permute-start(f32[128,384]{1,0:T(8,128)S(1)} %copy.361), channel_id=1, source_target_pairs={{0,1},{1,0},{2,3},{3,2},{4,5},{5,4},{6,7},{7,6},{8,9},{9,8},{10,11... | collective-permute-start | bytes 589832 | tf_op jit(solution)/shard_map/ppermute | solution.py:10
  67.0 7.1 %collective-permute-start.6 = (f32[128,384]{1,0:T(8,128)}, f32[128,384]{1,0:T(8,128)S(1)}, u32[]{:S(2)}, u32[]{:S(2)}) collective-permute-start(f32[128,384]{1,0:T(8,128)} %copy.349), channel_id=1, source_target_pairs={{0,4},{1,5},{2,6},{3,7},{4,0},{5,1},{6,2},{7,3},{8,12},{9,13},{10,... | collective-permute-start | bytes 589832 | tf_op jit(solution)/shard_map/ppermute | solution.py:10
  67.5 126.9 %collective-permute-start.13 = (f32[128,384]{1,0:T(8,128)S(1)}, f32[128,384]{1,0:T(8,128)}, u32[]{:S(2)}, u32[]{:S(2)}) collective-permute-start(f32[128,384]{1,0:T(8,128)S(1)} %copy.359), channel_id=1, source_target_pairs={{0,2},{1,3},{2,0},{3,1},{4,6},{5,7},{6,4},{7,5},{8,10},{9,11},{10,... | collective-permute-start | bytes 589832 | tf_op jit(solution)/shard_map/ppermute | solution.py:10
  74.1 5.6 %collective-permute-start.11 = (f32[128,384]{1,0:T(8,128)S(1)}, f32[128,384]{1,0:T(8,128)S(1)}, u32[]{:S(2)}, u32[]{:S(2)}) collective-permute-start(f32[128,384]{1,0:T(8,128)S(1)} %copy-done.39), channel_id=1, source_target_pairs={{0,4},{1,5},{2,6},{3,7},{4,0},{5,1},{6,2},{7,3},{8,12},{9,13},{10,... | collective-permute-start | bytes 589832 | tf_op jit(solution)/shard_map/ppermute | solution.py:10
  79.8 112.6 %collective-permute-start.7 = (f32[128,384]{1,0:T(8,128)S(1)}, f32[128,384]{1,0:T(8,128)S(1)}, u32[]{:S(2)}, u32[]{:S(2)}) collective-permute-start(f32[128,384]{1,0:T(8,128)S(1)} %select_n.151), channel_id=1, source_target_pairs={{0,2},{1,3},{2,0},{3,1},{4,6},{5,7},{6,4},{7,5},{8,10},{9,11},{10,... | collective-permute-start | bytes 589832 | tf_op jit(solution)/shard_map/ppermute | solution.py:10
  191.3 6.4 %collective-permute-start.12 = (f32[128,384]{1,0:T(8,128)S(1)}, f32[128,384]{1,0:T(8,128)}, u32[]{:S(2)}, u32[]{:S(2)}) collective-permute-start(f32[128,384]{1,0:T(8,128)S(1)} %select_n.159), channel_id=1, source_target_pairs={{0,2},{1,3},{2,0},{3,1},{4,6},{5,7},{6,4},{7,5},{8,10},{9,11},{10,... | collective-permute-start | bytes 589832 | tf_op jit(solution)/shard_map/ppermute | solution.py:10
  193.8 6.4 %collective-permute-start.9 = (f32[128,384]{1,0:T(8,128)S(1)}, f32[128,384]{1,0:T(8,128)S(1)}, u32[]{:S(2)}, u32[]{:S(2)}) collective-permute-start(f32[128,384]{1,0:T(8,128)S(1)} %select_n.155), channel_id=1, source_target_pairs={{0,1},{1,0},{2,3},{3,2},{4,5},{5,4},{6,7},{7,6},{8,9},{9,8},{10,11... | collective-permute-start | bytes 589832 | tf_op jit(solution)/shard_map/ppermute | solution.py:10
  199.2 2.5 %collective-permute-start.14 = (f32[128,384]{1,0:T(8,128)S(1)}, f32[128,384]{1,0:T(8,128)S(1)}, u32[]{:S(2)}, u32[]{:S(2)}) collective-permute-start(f32[128,384]{1,0:T(8,128)S(1)} %select_n.163), channel_id=1, source_target_pairs={{0,1},{1,0},{2,3},{3,2},{4,5},{5,4},{6,7},{7,6},{8,9},{9,8},{10,11... | collective-permute-start | bytes 589832 | tf_op jit(solution)/shard_map/ppermute | solution.py:10
  (36 other events, 79.5 us)
Sparse Core Ops, SparseCore 0:
  59.0 130.6 all-reduce.1
where the time goes:
time: 211 us; the launch traced here: 210 us
  waiting for transfers between devices  125 us (59%)
  local copies, waits for them, and re-layouts  32.4 us (15%)
  between operations  15.4 us (7%)
  other arithmetic  12.8 us (6%)
  starting transfers between devices  12.6 us (6%)
  matrix products  12.6 us (6%)
    psum x1, waiting for transfers between devices, shards(): summed = lax.psum(weight_term, ('dp', 'seqhi', 'seqlo'))  109 us
    ppermute x16, waiting for transfers between devices, swapped(): return lax.ppermute(value, axis, pairs)  15.3 us
    ppermute x16, starting transfers between devices, swapped(): return lax.ppermute(value, axis, pairs)  12.6 us
  transfers between devices with their start and end apart: 17, of which 5 were waited for; matrix products, arithmetic and copies ran while one was open for 14% of the time, Pallas kernels for 0%

commit v1 on v0

--- a/solution.py
+++ b/solution.py
@@ -152,7 +152,7 @@
     weight_term = lax.dot_general(
         attended, cotan_local, (((0,), (0,)), ((), ())), preferred_element_type=jnp.float32
     )
-    summed = lax.psum(weight_term, ("dp", "seqhi", "seqlo"))
+    summed = jnp.sum(lax.all_gather(weight_term, ("dp", "seqhi", "seqlo")), axis=0)
     weight_gradient = lax.dynamic_slice_in_dim(summed, lax.axis_index("dp") * own_rows, own_rows, 0)
     backward = lax.dot_general(
         cotan_local, out_weight, (((1,), (1,)), ((), ())), preferred_element_type=jnp.float32

time: 211 us -> 188 us (0.89)
  waiting for transfers between devices: 125 us -> 86.3 us
  other arithmetic: 12.8 us -> 23.7 us
    psum x1 -> x0, waiting for transfers between devices: 109 us -> none  [shards(): summed = lax.psum(weight_term, ('dp', 'seqhi', 'seqlo'))]
    all_gather x0 -> x1, waiting for transfers between devices: none -> 72.3 us  [shards(): lax.all_gather(weight_term, ('dp', 'seqhi', 'seqlo'))]
    reduce_sum x0 -> x1, other arithmetic: none -> 7.26 us  [shards(): jnp.sum(lax.all_gather(weight_term, ('dp', 'seqhi', 'seqlo')), axis=0)]
    dot_general x4, matrix products: 1.06 us -> 4.12 us  [attend_back(): jnp.einsum('rhe,che->hrc', grad_heads, split_heads(value_block, head_coun...]
    reshape x4, local copies, waits for them, and re-layouts: 1.22 us -> 3.41 us  [attend_back(): value_piece = jnp.einsum('hrc,rhe->che', probabilities, grad_heads, prefe...]
    unnamed x91 -> x115, local copies, waits for them, and re-layouts: 3.07 us -> 4.59 us
  transfers between devices with their start and end apart: 17 -> 17, of which waited for: 5 -> 4; matrix products, arithmetic and copies ran while one was open for 14% -> 26% of each run, Pallas kernels for 0% -> 0%
where the time goes in v1:
time: 188 us; the launch traced here: 187 us
  waiting for transfers between devices  86.3 us (46%)
  local copies, waits for them, and re-layouts  34.3 us (18%)
  other arithmetic  23.7 us (13%)
  between operations  15.6 us (8%)
  starting transfers between devices  14.2 us (8%)
  matrix products  13 us (7%)
    all_gather x1, waiting for transfers between devices, shards(): lax.all_gather(weight_term, ('dp', 'seqhi', 'seqlo'))  72.3 us
    ppermute x16, starting transfers between devices, swapped(): return lax.ppermute(value, axis, pairs)  14.2 us
    ppermute x16, waiting for transfers between devices, swapped(): return lax.ppermute(value, axis, pairs)  14.1 us
    reduce_sum x1, other arithmetic, shards(): jnp.sum(lax.all_gather(weight_term, ('dp', 'seqhi', 'seqlo')), axis=0)  7.26 us
    unnamed x115, local copies, waits for them, and re-layouts  4.59 us
    dot_general x4, matrix products, attend_back(): jnp.einsum('rhe,che->hrc', grad_heads, split_heads(value_block, head_coun...  4.12 us
    reshape x12, local copies, waits for them, and re-layouts, spread_rows(): return widened.reshape((matrix.shape[0] * factor,) + matrix.shape[1:])  4.01 us
  transfers between devices with their start and end apart: 17, of which 4 were waited for; matrix products, arithmetic and copies ran while one was open for 26% of the time, Pallas kernels for 0%

profile of v1, /device:TPU:1, one launch (start us, length us, event | category | flops | bytes accessed | tf_op | source)
XLA Modules:
  0.0 187.2 jit_solution(14338804921474066812)
XLA Ops:
  7.2 1.2 reshape.433
  15.0 2.3 %collective-permute-start.1 = (bf16[128,384]{1,0:T(8,128)(2,1)}, bf16[128,384]{1,0:T(8,128)(2,1)S(1)}, u32[]{:S(2)}, u32[]{:S(2)}) collective-permute-start(bf16[128,384]{1,0:T(8,128)(2,1)} %fusion.34), channel_id=1, source_target_pairs={{0,2},{1,3},{2,0},{3,1},{4,6},{5,7},{6,4},{7,5},{8,10},{9,11},{10,... | collective-permute-start | bytes 294920 | tf_op jit(solution)/shard_map/ppermute | solution.py:10
  22.5 1.3 collective-permute-start.2
  26.6 1.0 copy.325
  28.2 1.0 copy.306
  31.1 1.0 copy.326
  33.8 1.5 reshape.410
  35.3 1.1 copy.330
  36.4 2.1 %divide_convert_fusion = (bf16[256,384]{1,0:T(8,128)(2,1)}, f32[256,384]{1,0:T(8,128)S(1)}) fusion(f32[256,384]{1,0:T(8,128)} %copy.314, bf16[384,384]{1,0:T(8,128)(2,1)S(1)} %copy-done, bf16[1,256,384]{2,1,0:T(8,128)(2,1)} %param.11), kind=kOutput, calls=%fused_computation.35 | convolution fusion | flops 75890688 | bytes 1474560 | tf_op jit(solution)/shard_map/dot_general | solution.py:157
  38.7 1.3 fusion.57
  40.0 1.1 fusion.30
  42.9 1.2 div.50.clone
  44.2 1.2 div.55
  45.3 1.9 %divide_reduce_fusion = f32[128,384]{1,0:T(8,128)S(1)} fusion(f32[128,2,384]{2,1,0:T(2,128)} %reshape.442, f32[128,2,384]{2,1,0:T(2,128)} %div.55), kind=kLoop, calls=%fused_computation.36 | loop fusion | flops 147456 | bytes 983040 | tf_op jit(solution)/shard_map/reduce_sum | solution.py:33
  49.0 1.3 collective-permute-start.11
  51.4 1.2 collective-permute-start.13
  53.9 2.9 %collective-permute-start.15 = (f32[128,384]{1,0:T(8,128)}, f32[128,384]{1,0:T(8,128)}, u32[]{:S(2)}, u32[]{:S(2)}) collective-permute-start(f32[128,384]{1,0:T(8,128)} %copy.361), channel_id=1, source_target_pairs={{0,1},{1,0},{2,3},{3,2},{4,5},{5,4},{6,7},{7,6},{8,9},{9,8},{10,11... | collective-permute-start | bytes 589832 | tf_op jit(solution)/shard_map/ppermute | solution.py:10
  63.0 1.1 fusion.10
  68.1 1.1 multiply_convert_fusion
  74.7 1.8 collective-permute-start.12
  78.1 7.8 %collective-permute-done.12 = f32[128,384]{1,0:T(8,128)S(1)} collective-permute-done((f32[128,384]{1,0:T(8,128)S(1)}, f32[128,384]{1,0:T(8,128)S(1)}, u32[]{:S(2)}, u32[]{:S(2)}) %collective-permute-start.12) | collective-permute-done | bytes 196640 | tf_op jit(solution)/shard_map/ppermute | solution.py:10
  88.3 6.1 %collective-permute-done.7 = f32[128,384]{1,0:T(8,128)S(1)} collective-permute-done((f32[128,384]{1,0:T(8,128)S(1)}, f32[128,384]{1,0:T(8,128)S(1)}, u32[]{:S(2)}, u32[]{:S(2)}) %collective-permute-start.7) | collective-permute-done | bytes 196640 | tf_op jit(solution)/shard_map/ppermute | solution.py:10
  100.1 72.3 %all-gather.3.cloned.1.call-done = f32[12288,384]{1,0:T(8,128)} async-done(((f32[384,384]{1,0:T(8,128)}), f32[12288,384]{1,0:T(8,128)}) %all-gather.3.cloned.1.call-update) | async-done | bytes 18874384 | tf_op jit(solution)/shard_map/all_gather | solution.py:155
  172.4 7.3 %reduce_sum.119 = f32[384,384]{1,0:T(8,128)S(1)} reduce(f32[32,384,384]{2,1,0:T(8,128)} %bitcast.148, f32[]{:T(128)} %constant.67.clone.1), dimensions={0}, to_apply=%region_11.12 | reduce | flops 4571136 | bytes 19464196 | tf_op jit(solution)/shard_map/reduce_sum | solution.py:155
  (303 shorter events, 49.4 us)
Async XLA Ops:
  7.2 29.2 %copy-start = (bf16[384,384]{1,0:T(8,128)(2,1)S(1)}, bf16[384,384]{1,0:T(8,128)(2,1)}, u32[]{:S(2)}) copy-start(bf16[384,384]{1,0:T(8,128)(2,1)} %param.10) | copy-start | bytes 884740
  7.2 165.2 %all-gather.3.cloned.1.call-start = ((), (), s32[]{:S(2)}) async-start(), calls=%async_computation | async-start | bytes 19464192 | tf_op jit(solution)/shard_map/all_gather | solution.py:155
  8.8 4.8 %collective-permute-start = (bf16[128,384]{1,0:T(8,128)(2,1)S(1)}, bf16[128,384]{1,0:T(8,128)(2,1)S(1)}, u32[]{:S(2)}, u32[]{:S(2)}) collective-permute-start(bf16[128,384]{1,0:T(8,128)(2,1)S(1)} %fusion.33), channel_id=1, source_target_pairs={{0,1},{1,0},{2,3},{3,2},{4,5},{5,4},{6,7},{7,6},{8,9},{9,8},{10,11... | collective-permute-start | bytes 294920 | tf_op jit(solution)/shard_map/ppermute | solution.py:10
  9.5 4.1 %collective-permute-start.3 = (bf16[128,384]{1,0:T(8,128)(2,1)S(1)}, bf16[128,384]{1,0:T(8,128)(2,1)S(1)}, u32[]{:S(2)}, u32[]{:S(2)}) collective-permute-start(bf16[128,384]{1,0:T(8,128)(2,1)S(1)} %fusion.36), channel_id=1, source_target_pairs={{0,1},{1,0},{2,3},{3,2},{4,5},{5,4},{6,7},{7,6},{8,9},{9,8},{10,11... | collective-permute-start | bytes 294920 | tf_op jit(solution)/shard_map/ppermute | solution.py:10
  10.8 7.9 %copy-start.23 = (bf16[128,1,384]{0,2,1:T(8,128)(2,1)}, bf16[128,1,384]{0,2,1:T(8,128)(2,1)S(1)}, u32[]{:S(2)}) copy-start(bf16[128,1,384]{0,2,1:T(8,128)(2,1)S(1)} %copy.296) | copy-start | bytes 294916
  12.0 17.2 %copy-start.53 = (f32[6]{0:T(128)}, f32[6]{0:T(128)S(1)}, u32[]{:S(2)}) copy-start(f32[6]{0:T(128)S(1)} %broadcast_multiply_fusion.1) | copy-start | bytes 76
  13.5 15.8 %copy-start.36 = (bf16[32,6,64]{2,1,0:T(8,128)(2,1)}, bf16[32,6,64]{2,1,0:T(8,128)(2,1)S(1)}, u32[]{:S(2)}) copy-start(bf16[32,6,64]{2,1,0:T(8,128)(2,1)S(1)} %convert_element_type.251) | copy-start | bytes 73732
  13.6 12.6 %copy-start.10 = (bf16[64,384]{0,1:T(8,128)(2,1)}, bf16[64,384]{0,1:T(8,128)(2,1)S(1)}, u32[]{:S(2)}) copy-start(bf16[64,384]{0,1:T(8,128)(2,1)S(1)} %copy.389) | copy-start | bytes 147460
  15.0 5.3 %collective-permute-start.1 = (bf16[128,384]{1,0:T(8,128)(2,1)}, bf16[128,384]{1,0:T(8,128)(2,1)S(1)}, u32[]{:S(2)}, u32[]{:S(2)}) collective-permute-start(bf16[128,384]{1,0:T(8,128)(2,1)} %fusion.34), channel_id=1, source_target_pairs={{0,2},{1,3},{2,0},{3,1},{4,6},{5,7},{6,4},{7,5},{8,10},{9,11},{10,... | collective-permute-start | bytes 294920 | tf_op jit(solution)/shard_map/ppermute | solution.py:10
  18.6 5.2 %collective-permute-start.4 = (bf16[128,384]{1,0:T(8,128)(2,1)}, bf16[128,384]{1,0:T(8,128)(2,1)S(1)}, u32[]{:S(2)}, u32[]{:S(2)}) collective-permute-start(bf16[128,384]{1,0:T(8,128)(2,1)} %fusion.37), channel_id=1, source_target_pairs={{0,2},{1,3},{2,0},{3,1},{4,6},{5,7},{6,4},{7,5},{8,10},{9,11},{10,... | collective-permute-start | bytes 294920 | tf_op jit(solution)/shard_map/ppermute | solution.py:10
  22.5 5.7 %collective-permute-start.2 = (bf16[128,384]{1,0:T(8,128)(2,1)}, bf16[128,384]{1,0:T(8,128)(2,1)}, u32[]{:S(2)}, u32[]{:S(2)}) collective-permute-start(bf16[128,384]{1,0:T(8,128)(2,1)} %fusion.35), channel_id=1, source_target_pairs={{0,4},{1,5},{2,6},{3,7},{4,0},{5,1},{6,2},{7,3},{8,12},{9,13},{10,... | collective-permute-start | bytes 294920 | tf_op jit(solution)/shard_map/ppermute | solution.py:10
  25.9 5.2 %collective-permute-start.5 = (bf16[128,384]{1,0:T(8,128)(2,1)}, bf16[128,384]{1,0:T(8,128)(2,1)}, u32[]{:S(2)}, u32[]{:S(2)}) collective-permute-start(bf16[128,384]{1,0:T(8,128)(2,1)} %bitcast.147), channel_id=1, source_target_pairs={{0,4},{1,5},{2,6},{3,7},{4,0},{5,1},{6,2},{7,3},{8,12},{9,13},{10,... | collective-permute-start | bytes 294920 | tf_op jit(solution)/shard_map/ppermute | solution.py:10
  47.8 8.9 %copy-start.50 = (bf16[256,384]{1,0:T(8,128)(2,1)S(1)}, bf16[256,384]{1,0:T(8,128)(2,1)}, u32[]{:S(2)}) copy-start(bf16[256,384]{1,0:T(8,128)(2,1)} %get-tuple-element.44) | copy-start | bytes 589828
  49.0 24.0 %collective-permute-start.11 = (f32[128,384]{1,0:T(8,128)}, f32[128,384]{1,0:T(8,128)}, u32[]{:S(2)}, u32[]{:S(2)}) collective-permute-start(f32[128,384]{1,0:T(8,128)} %copy.357), channel_id=1, source_target_pairs={{0,4},{1,5},{2,6},{3,7},{4,0},{5,1},{6,2},{7,3},{8,12},{9,13},{10,... | collective-permute-start | bytes 589832 | tf_op jit(solution)/shard_map/ppermute | solution.py:10
  51.4 26.5 %collective-permute-start.13 = (f32[128,384]{1,0:T(8,128)}, f32[128,384]{1,0:T(8,128)}, u32[]{:S(2)}, u32[]{:S(2)}) collective-permute-start(f32[128,384]{1,0:T(8,128)} %copy.359), channel_id=1, source_target_pairs={{0,2},{1,3},{2,0},{3,1},{4,6},{5,7},{6,4},{7,5},{8,10},{9,11},{10,... | collective-permute-start | bytes 589832 | tf_op jit(solution)/shard_map/ppermute | solution.py:10
  53.9 42.7 %collective-permute-start.15 = (f32[128,384]{1,0:T(8,128)}, f32[128,384]{1,0:T(8,128)}, u32[]{:S(2)}, u32[]{:S(2)}) collective-permute-start(f32[128,384]{1,0:T(8,128)} %copy.361), channel_id=1, source_target_pairs={{0,1},{1,0},{2,3},{3,2},{4,5},{5,4},{6,7},{7,6},{8,9},{9,8},{10,11... | collective-permute-start | bytes 589832 | tf_op jit(solution)/shard_map/ppermute | solution.py:10
  58.3 7.8 %copy-start.30 = (bf16[128,384]{0,1:T(8,128)(2,1)S(1)}, bf16[128,384]{0,1:T(8,128)(2,1)}, u32[]{:S(2)}) copy-start(bf16[128,384]{0,1:T(8,128)(2,1)} %copy-done.29) | copy-start | bytes 294916
  61.8 12.9 %collective-permute-start.6 = (f32[128,384]{1,0:T(8,128)}, f32[128,384]{1,0:T(8,128)}, u32[]{:S(2)}, u32[]{:S(2)}) collective-permute-start(f32[128,384]{1,0:T(8,128)} %copy.349), channel_id=1, source_target_pairs={{0,4},{1,5},{2,6},{3,7},{4,0},{5,1},{6,2},{7,3},{8,12},{9,13},{10,... | collective-permute-start | bytes 589832 | tf_op jit(solution)/shard_map/ppermute | solution.py:10
  65.2 23.1 %collective-permute-start.8 = (f32[128,384]{1,0:T(8,128)}, f32[128,384]{1,0:T(8,128)}, u32[]{:S(2)}, u32[]{:S(2)}) collective-permute-start(f32[128,384]{1,0:T(8,128)} %copy.351), channel_id=1, source_target_pairs={{0,2},{1,3},{2,0},{3,1},{4,6},{5,7},{6,4},{7,5},{8,10},{9,11},{10,... | collective-permute-start | bytes 589832 | tf_op jit(solution)/shard_map/ppermute | solution.py:10
  73.1 24.9 %collective-permute-start.10 = (f32[128,384]{1,0:T(8,128)S(1)}, f32[128,384]{1,0:T(8,128)S(1)}, u32[]{:S(2)}, u32[]{:S(2)}) collective-permute-start(f32[128,384]{1,0:T(8,128)S(1)} %copy-done.49), channel_id=1, source_target_pairs={{0,1},{1,0},{2,3},{3,2},{4,5},{5,4},{6,7},{7,6},{8,9},{9,8},{10,11... | collective-permute-start | bytes 589832 | tf_op jit(solution)/shard_map/ppermute | solution.py:10
  74.7 11.2 %collective-permute-start.12 = (f32[128,384]{1,0:T(8,128)S(1)}, f32[128,384]{1,0:T(8,128)S(1)}, u32[]{:S(2)}, u32[]{:S(2)}) collective-permute-start(f32[128,384]{1,0:T(8,128)S(1)} %select_n.159), channel_id=1, source_target_pairs={{0,2},{1,3},{2,0},{3,1},{4,6},{5,7},{6,4},{7,5},{8,10},{9,11},{10,... | collective-permute-start | bytes 589832 | tf_op jit(solution)/shard_map/ppermute | solution.py:10
  78.0 16.3 %collective-permute-start.7 = (f32[128,384]{1,0:T(8,128)S(1)}, f32[128,384]{1,0:T(8,128)S(1)}, u32[]{:S(2)}, u32[]{:S(2)}) collective-permute-start(f32[128,384]{1,0:T(8,128)S(1)} %select_n.151), channel_id=1, source_target_pairs={{0,2},{1,3},{2,0},{3,1},{4,6},{5,7},{6,4},{7,5},{8,10},{9,11},{10,... | collective-permute-start | bytes 589832 | tf_op jit(solution)/shard_map/ppermute | solution.py:10
  87.1 9.4 %collective-permute-start.14 = (f32[128,384]{1,0:T(8,128)S(1)}, f32[128,384]{1,0:T(8,128)S(1)}, u32[]{:S(2)}, u32[]{:S(2)}) collective-permute-start(f32[128,384]{1,0:T(8,128)S(1)} %select_n.163), channel_id=1, source_target_pairs={{0,1},{1,0},{2,3},{3,2},{4,5},{5,4},{6,7},{7,6},{8,9},{9,8},{10,11... | collective-permute-start | bytes 589832 | tf_op jit(solution)/shard_map/ppermute | solution.py:10
  95.5 2.4 %collective-permute-start.9 = (f32[128,384]{1,0:T(8,128)S(1)}, f32[128,384]{1,0:T(8,128)S(1)}, u32[]{:S(2)}, u32[]{:S(2)}) collective-permute-start(f32[128,384]{1,0:T(8,128)S(1)} %select_n.155), channel_id=1, source_target_pairs={{0,1},{1,0},{2,3},{3,2},{4,5},{5,4},{6,7},{7,6},{8,9},{9,8},{10,11... | collective-permute-start | bytes 589832 | tf_op jit(solution)/shard_map/ppermute | solution.py:10
  (48 other events, 115.0 us)
Sparse Core Ops, SparseCore 0:
  41.2 131.0 all-gather.2
